TPU v7x, 512 devices: a whole 4x4x16 slice. The times are simulated.
512 devices in a mesh: pix: 32 (over z, core), tm: 16 (over y, x).
Axes of the slice: x: 4, y: 4, z: 16, core: 2. Of those that a mesh axis runs over, the one named last changes fastest.
Arguments:
- raw_frames: bfloat16 [1024, 262144], P('tm', 'pix'), may hold values from 0.099609375 to 4
- eigen_flats: bfloat16 [16, 262144], P(None, 'pix'), may hold values from 0 to 1
- weights: float32 [1024, 16], P('tm'), may hold values from 0.02 to 1
- flat_count: int32 [1024], P('tm'), may hold values from 1 to 16
- bin_map: int32 [262144], P('pix'), may hold values from 0 to 64, as said below
Outputs:
- two_time: float32 [64, 1024, 1024], P('pix', 'tm')
Inputs may be any that keep to these rules, and one draw needn't show every extreme that they name: `bin_map`: each block of 8192 pixels (one device's tile) holds 60 to 96 pixels of every bin 1 to 64; in every draw one bin holds exactly 96 pixels in every tile.
All inputs are finite; a program needn't handle non-finite values.
Results may differ from a plain program's by a relative error of at most 0.0003.
Values may be sent and summed in bfloat16 or wider, within the bound.
No kernel may reach another device: no remote copies, remote signals or barrier semaphores. Data moves between devices by JAX's collectives and lax.ppermute only.
A program may use at most 64 MiB of HBM per device.

v0:
```python
import jax
import jax.numpy as jnp
from jax import lax
from jax.sharding import PartitionSpec as P

CAP = 96
BIN_DEV = 2


def bin_block(own_frames, local_sums, pixel_counts, portion):
    products = jnp.einsum("tsbc,usbc->btu", own_frames, portion, preferred_element_type=jnp.float32)
    other_sums = jnp.transpose(jnp.sum(portion, axis=(1, 3), dtype=jnp.float32))
    scaled = pixel_counts[:, None, None] * products
    return scaled / (local_sums[:, :, None] * other_sums[:, None, :])


def shards(raw_frames, eigen_flats, weights, flat_count, bin_map):
    frames, pixels = raw_frames.shape
    eigen_count = eigen_flats.shape[0]
    in_use = lax.broadcasted_iota(jnp.int32, (frames, eigen_count), 1) < flat_count[:, None]
    coefficients = jnp.where(in_use, weights, 0.0)
    flat_field = 0.5 + jnp.dot(
        coefficients, eigen_flats.astype(jnp.float32), precision=lax.Precision.HIGHEST
    )
    corrected = (raw_frames.astype(jnp.float32) / flat_field).astype(jnp.bfloat16)
    owners = lax.axis_size("pix")
    bin_total = BIN_DEV * owners
    labels = jnp.where(bin_map > 0, bin_map - 1, bin_total)
    ordering = jnp.argsort(labels * pixels + jnp.arange(pixels, dtype=jnp.int32))
    member = labels[:, None] == jnp.arange(bin_total, dtype=jnp.int32)[None, :]
    counts = jnp.sum(member, axis=0, dtype=jnp.int32)
    starts = jnp.cumsum(counts) - counts
    slot_index = jnp.arange(CAP, dtype=jnp.int32)
    filled = slot_index[None, :] < counts[:, None]
    source = ordering[jnp.minimum(starts[:, None] + slot_index[None, :], pixels - 1)]
    packed = jnp.where(
        filled.reshape(-1)[None, :], corrected[:, source.reshape(-1)], jnp.zeros((), jnp.bfloat16)
    )
    tallies = counts.astype(jnp.bfloat16)[None, :]
    received, tally_in = (
        lax.all_to_all(packed, "pix", split_axis=1, concat_axis=1, tiled=True),
        lax.all_to_all(tallies, "pix", split_axis=1, concat_axis=1, tiled=True),
    )
    own_frames = received.reshape(frames, owners, BIN_DEV, CAP)
    pixel_counts = jnp.sum(tally_in.astype(jnp.float32).reshape(owners, BIN_DEV), axis=0)
    local_sums = jnp.transpose(jnp.sum(own_frames, axis=(1, 3), dtype=jnp.float32))
    return bin_block(
        own_frames, local_sums, pixel_counts, lax.all_gather(own_frames, "tm", axis=0, tiled=True)
    )


def solution(mesh):
    return jax.shard_map(
        shards,
        mesh=mesh,
        in_specs=(P("tm", "pix"), P(None, "pix"), P("tm", None), P("tm"), P("pix")),
        out_specs=P("pix", "tm", None),
        check_vma=False,
    )
```

profile of v0, /device:TPU:1, one launch (start us, length us, event | category | flops | bytes accessed | tf_op | source)
XLA Modules:
  0.0 294.0 jit_solution(1987480666871033830)
XLA Ops:
  6.6 0.8 add_select_fusion
  7.4 0.3 convert_reduce_fusion.2
  7.7 0.1 lt.61
  7.8 0.1 lt.62
  8.0 0.1 copy.28
  8.1 0.1 reduce-window.8
  8.2 0.1 reduce.3
  8.5 6.8 %sort.17 = (s32[8192]{0:T(1024)}, s32[8192]{0:T(1024)S(1)}) sort(s32[8192]{0:T(1024)S(1)} %get-tuple-element.8, s32[8192]{0:T(1024)S(1)} %iota.25), dimensions={0}, to_apply=%region_2.3 | sort | flops 106496 | bytes 131072 | tf_op jit(solution)/shard_map/jit(argsort)/sort | solution.py:29
  15.3 34.3 %gather_fusion = s32[6144]{0:T(1024)S(1)} fusion(s32[8192]{0:T(1024)S(1)} %get-tuple-element.6, s32[6144]{0:T(1024)S(1)} %broadcast_clamp_fusion), kind=kCustom, calls=%fused_computation | custom fusion | bytes 73728 | tf_op jit(solution)/shard_map/gather | solution.py:35
  49.7 1.2 fusion.1
  50.9 1.1 copy.29
  52.0 22.1 %gather_fusion.1 = bf16[6144,64]{1,0:T(8,128)(2,1)} fusion(bf16[64,8192]{0,1:T(8,128)(2,1)S(1)} %copy.29, s32[6144]{0:T(1024)S(1)} %broadcast_clamp_fusion.1), kind=kCustom, calls=%fused_computation.1 | custom fusion | bytes 1597440 | tf_op jit(solution)/shard_map/gather | solution.py:37
  74.0 1.8 copy.30
  76.0 72.2 %all_to_all.12 = bf16[64,32,192]{2,0,1:T(8,128)(2,1)S(1)} all-to-all(bf16[64,32,192]{2,0,1:T(8,128)(2,1)S(1)} %broadcast_select_fusion), channel_id=1, replica_groups=mesh['pix'=32,'tm'=16] {'pix'}, dimensions={1} | all-to-all | bytes 1572864 | tf_op jit(solution)/shard_map/all_to_all | solution.py:41
  148.2 0.6 reshape.176
  148.8 1.3 copy.33
  150.1 0.1 convert_element_type.46
  150.2 15.1 %all_to_all.13 = bf16[1,32,2]{2,0,1:T(2,128)(2,1)S(1)} all-to-all(bf16[1,32,2]{2,0,1:T(2,128)(2,1)S(1)} %convert_element_type.46), channel_id=1, replica_groups=mesh['pix'=32,'tm'=16] {'pix'}, dimensions={1} | all-to-all | bytes 256 | tf_op jit(solution)/shard_map/all_to_all | solution.py:42
  165.3 0.2 convert_reduce_fusion.1
  165.5 0.1 reduce_sum.46
  165.6 0.1 reduce_sum.47
  165.8 102.4 %all-gather.2.cloned.1.call-done = bf16[1024,32,2,96]{3,0,1,2:T(8,128)(2,1)} async-done(((bf16[64,32,2,96]{3,0,1,2:T(8,128)(2,1)}), bf16[1024,32,2,96]{3,0,1,2:T(8,128)(2,1)}) %all-gather.2.cloned.1.call-update) | async-done | bytes 12582928 | tf_op jit(solution)/shard_map/all_gather | solution.py:48
  268.2 7.2 %convert_reduce_fusion = f32[1024,2]{0,1:T(2,128)S(1)} fusion(bf16[1024,32,2,96]{3,0,1,2:T(8,128)(2,1)} %all-gather.2.cloned.1.call-done), kind=kLoop, calls=%fused_computation.2 | loop fusion | flops 12580864 | bytes 12591104 | tf_op jit(solution)/shard_map/reduce_sum | solution.py:12
  275.5 11.7 %fusion.3 = f32[2,64,1024]{2,1,0:T(8,128)} fusion(bf16[1024,32,2,96]{3,0,1,2:T(8,128)(2,1)} %all-gather.2.cloned.1.call-done, f32[2,1024]{1,0:T(2,128)S(1)} %bitcast.24, f32[2,64]{1,0:T(2,128)S(1)} %bitcast.25, f32[2]{0:T(128)S(1)} %convert_reduce_fusion.3, bf16[64,32,2,96]{3,2,0,1:T(2,128)(2,1)S(1)} %reshape.176), kind=kOutput, calls=%fused_computation.11 | convolution fusion | flops 805699584 | bytes 13902344 | tf_op jit(solution)/shard_map/tsbc,usbc->btu/dot_general | solution.py:11
  (24 shorter events, 0.6 us)
Async XLA Ops:
  6.5 43.1 %copy-start = (bf16[16,8192]{1,0:T(8,128)(2,1)S(1)}, bf16[16,8192]{1,0:T(8,128)(2,1)}, u32[]{:S(2)}) copy-start(bf16[16,8192]{1,0:T(8,128)(2,1)} %param.6) | copy-start | bytes 786436
  6.5 261.7 %all-gather.2.cloned.1.call-start = ((), (), s32[]{:S(2)}) async-start(), calls=%async_computation.2 | async-start | bytes 17825792 | tf_op jit(solution)/shard_map/all_gather | solution.py:48
  15.3 34.4 %copy-start.1 = (bf16[64,8192]{1,0:T(8,128)(2,1)S(1)}, bf16[64,8192]{1,0:T(8,128)(2,1)}, u32[]{:S(2)}) copy-start(bf16[64,8192]{1,0:T(8,128)(2,1)} %param.5) | copy-start | bytes 3145732
  15.3 34.4 %copy-start.2 = (f32[64,16]{0,1:T(8,128)S(1)}, f32[64,16]{0,1:T(8,128)}, u32[]{:S(2)}) copy-start(f32[64,16]{0,1:T(8,128)} %param.7) | copy-start | bytes 12292
  15.3 34.4 %copy-start.3 = (s32[64]{0:T(128)S(1)}, s32[64]{0:T(128)}, u32[]{:S(2)}) copy-start(s32[64]{0:T(128)} %param.8) | copy-start | bytes 772
Sparse Core Ops, SparseCore 0:
  150.2 118.0 all-gather.1
where the time goes:
time: 294 us
  waiting for transfers between devices  102 us (35%)
  blocking collectives  87.3 us (30%)
  local copies, waits for them, and re-layouts  61.9 us (21%)
  other arithmetic  15.9 us (5%)
  between operations  13.6 us (5%)
  matrix products  12.9 us (4%)
    all_gather x1, waiting for transfers between devices, shards(): lax.all_gather(own_frames, 'tm', axis=0, tiled=True)  102 us
    all_to_all x1, blocking collectives, shards(): lax.all_to_all(packed, 'pix', split_axis=1, concat_axis=1, tiled=True)  72.2 us
    gather x1, local copies, waits for them, and re-layouts, shards(): ordering[jnp.minimum(starts[:, None] + slot_index[None, :], pixels - 1)]  34.3 us
    gather x2, local copies, waits for them, and re-layouts, shards(): corrected[:, source.reshape(-1)]  23.9 us
    all_to_all x1, blocking collectives, shards(): lax.all_to_all(tallies, 'pix', split_axis=1, concat_axis=1, tiled=True)  15.1 us
    dot_general x1, matrix products, bin_block(): jnp.einsum('tsbc,usbc->btu', own_frames, portion, preferred_element_type=...  11.7 us
    reduce_sum x1, other arithmetic, bin_block(): other_sums = jnp.transpose(jnp.sum(portion, axis=(1, 3), dtype=jnp.float32))  7.24 us
    sort x1, other arithmetic, shards(): jnp.argsort(labels * pixels + jnp.arange(pixels, dtype=jnp.int32))  6.77 us
  transfers between devices with their start and end apart: 1, of which 1 were waited for; matrix products, arithmetic and copies ran while one was open for 0% of the time, Pallas kernels for 0%

commit v1 on v0

--- a/solution.py
+++ b/solution.py
@@ -45,7 +45,12 @@
     pixel_counts = jnp.sum(tally_in.astype(jnp.float32).reshape(owners, BIN_DEV), axis=0)
     local_sums = jnp.transpose(jnp.sum(own_frames, axis=(1, 3), dtype=jnp.float32))
     return bin_block(
-        own_frames, local_sums, pixel_counts, lax.all_gather(own_frames, "tm", axis=0, tiled=True)
+        own_frames,
+        local_sums,
+        pixel_counts,
+        jnp.concatenate(
+            lax.all_to_all(jnp.stack([own_frames] * lax.axis_size("tm")), "tm", 0, 0), axis=0
+        ),
     )
 
 

time: 294 us -> 442 us (1.50)
  waiting for transfers between devices: 102 us -> 312 us
  blocking collectives: 87.3 us -> 0 us
  starting transfers between devices: 0.01 us -> 27.6 us
  between operations: 13.6 us -> 0.22 us
  local copies, waits for them, and re-layouts: 61.9 us -> 68.9 us
    all_to_all x0 -> x3, waiting for transfers between devices: none -> 312 us  [the longest x1 247 us: shards(): lax.all_to_all(jnp.stack([own_frames] * lax.axis_size('tm')), 'tm', 0, 0)]
    all_gather x1 -> x0, waiting for transfers between devices: 102 us -> none  [shards(): lax.all_gather(own_frames, 'tm', axis=0, tiled=True)]
    all_to_all x2 -> x0, blocking collectives: 87.3 us -> none  [the longest x1 72.2 us: shards(): lax.all_to_all(packed, 'pix', split_axis=1, concat_axis=1, tiled=True)]
    all_to_all x0 -> x3, starting transfers between devices: none -> 27.6 us  [the longest x1 16.7 us: shards(): lax.all_to_all(packed, 'pix', split_axis=1, concat_axis=1, tiled=True)]
    another operation x1 -> x2, local copies, waits for them, and re-layouts: 0.1 us -> 6.31 us  [the longest x1 6.21 us: shards(): jnp.stack([own_frames] * lax.axis_size('tm'))]
  transfers between devices with their start and end apart: 1 -> 3, of which waited for: 1 -> 3; matrix products, arithmetic and copies ran while one was open for 0% -> 1% of each run, Pallas kernels for 0% -> 0%
where the time goes in v1:
time: 442 us
  waiting for transfers between devices  312 us (71%)
  local copies, waits for them, and re-layouts  68.9 us (16%)
  starting transfers between devices  27.6 us (6%)
  other arithmetic  17.7 us (4%)
  matrix products  15.1 us (3%)
    all_to_all x1, waiting for transfers between devices, shards(): lax.all_to_all(jnp.stack([own_frames] * lax.axis_size('tm')), 'tm', 0, 0)  247 us
    all_to_all x1, waiting for transfers between devices, shards(): lax.all_to_all(packed, 'pix', split_axis=1, concat_axis=1, tiled=True)  55 us
    gather x1, local copies, waits for them, and re-layouts, shards(): ordering[jnp.minimum(starts[:, None] + slot_index[None, :], pixels - 1)]  34.3 us
    gather x2, local copies, waits for them, and re-layouts, shards(): corrected[:, source.reshape(-1)]  23.9 us
    all_to_all x1, starting transfers between devices, shards(): lax.all_to_all(packed, 'pix', split_axis=1, concat_axis=1, tiled=True)  16.7 us
    dot_general x1, matrix products, bin_block(): jnp.einsum('tsbc,usbc->btu', own_frames, portion, preferred_element_type=...  13.9 us
    all_to_all x1, waiting for transfers between devices, shards(): lax.all_to_all(tallies, 'pix', split_axis=1, concat_axis=1, tiled=True)  9.98 us
  transfers between devices with their start and end apart: 3, of which 3 were waited for; matrix products, arithmetic and copies ran while one was open for 1% of the time, Pallas kernels for 0%

profile of v1, /device:TPU:1, one launch (start us, length us, event | category | flops | bytes accessed | tf_op | source)
XLA Modules:
  0.0 442.0 jit_solution(8283958780587698102)
XLA Ops:
  0.1 0.8 add_select_fusion
  0.9 0.3 convert_reduce_fusion.2
  2.0 6.8 %sort.17 = (s32[8192]{0:T(1024)}, s32[8192]{0:T(1024)S(1)}) sort(s32[8192]{0:T(1024)S(1)} %get-tuple-element.8, s32[8192]{0:T(1024)S(1)} %iota.25), dimensions={0}, to_apply=%region_2.3 | sort | flops 106496 | bytes 131072 | tf_op jit(solution)/shard_map/jit(argsort)/sort | solution.py:29
  8.8 34.3 %gather_fusion = s32[6144]{0:T(1024)S(1)} fusion(s32[8192]{0:T(1024)S(1)} %get-tuple-element.6, s32[6144]{0:T(1024)S(1)} %broadcast_clamp_fusion), kind=kCustom, calls=%fused_computation | custom fusion | bytes 73728 | tf_op jit(solution)/shard_map/gather | solution.py:35
  43.1 1.2 fusion.3
  44.3 1.1 copy.35
  45.4 22.1 %gather_fusion.1 = bf16[6144,64]{1,0:T(8,128)(2,1)} fusion(bf16[64,8192]{0,1:T(8,128)(2,1)S(1)} %copy.35, s32[6144]{0:T(1024)S(1)} %broadcast_clamp_fusion.1), kind=kCustom, calls=%fused_computation.1 | custom fusion | bytes 1597440 | tf_op jit(solution)/shard_map/gather | solution.py:37
  67.5 1.8 copy.36
  69.3 1.1 broadcast_select_fusion
  70.4 16.7 %all-to-all-start.1 = ((bf16[64,32,192]{2,0,1:T(8,128)(2,1)}), bf16[64,32,192]{2,0,1:T(8,128)(2,1)S(1)}, u32[]{:S(2)}, u32[]{:S(2)}) async-start(bf16[64,32,192]{2,0,1:T(8,128)(2,1)} %broadcast_select_fusion), calls=%async_computation.1 | async-start | bytes 2097152 | tf_op jit(solution)/shard_map/all_to_all | solution.py:41
  87.1 0.7 convert_element_type.47
  87.9 55.0 %all-to-all-done.1 = bf16[64,32,192]{2,0,1:T(8,128)(2,1)S(1)} async-done(((bf16[64,32,192]{2,0,1:T(8,128)(2,1)}), bf16[64,32,192]{2,0,1:T(8,128)(2,1)S(1)}, u32[]{:S(2)}, u32[]{:S(2)}) %all-to-all-start.1) | async-done | bytes 786464 | tf_op jit(solution)/shard_map/all_to_all | solution.py:41
  142.8 4.0 all-to-all-start
  146.9 0.6 reshape.184
  147.5 1.2 copy.38
  148.7 10.0 %all-to-all-done = bf16[1,32,2]{2,0,1:T(2,128)(2,1)S(1)} async-done(((bf16[1,32,2]{2,0,1:T(2,128)(2,1)}), bf16[1,32,2]{2,0,1:T(2,128)(2,1)S(1)}, u32[]{:S(2)}, u32[]{:S(2)}) %all-to-all-start) | async-done | bytes 160 | tf_op jit(solution)/shard_map/all_to_all | solution.py:42
  158.7 6.2 %stack.3 = bf16[16,64,32,2,96]{4,2,3,1,0:T(8,128)(2,1)} broadcast(bf16[64,32,2,96]{3,1,2,0:T(8,128)(2,1)S(1)} %copy.38), dimensions={1,2,3,4} | broadcast | bytes 13369344 | tf_op jit(solution)/shard_map/stack | solution.py:52
  164.9 6.8 %all-to-all-start.2 = ((bf16[16,64,32,2,96]{4,2,3,1,0:T(8,128)(2,1)}), bf16[16,64,32,2,96]{4,2,3,1,0:T(8,128)(2,1)}, u32[]{:S(2)}, u32[]{:S(2)}) async-start(bf16[16,64,32,2,96]{4,2,3,1,0:T(8,128)(2,1)} %stack.3), calls=%async_computation.2 | async-start | bytes 33554432 | tf_op jit(solution)/shard_map/all_to_all | solution.py:52
  171.8 0.2 convert_reduce_fusion.1
  172.1 0.1 reduce_sum.49
  172.3 247.5 %all-to-all-done.2 = bf16[16,64,32,2,96]{4,2,3,1,0:T(8,128)(2,1)} async-done(((bf16[16,64,32,2,96]{4,2,3,1,0:T(8,128)(2,1)}), bf16[16,64,32,2,96]{4,2,3,1,0:T(8,128)(2,1)}, u32[]{:S(2)}, u32[]{:S(2)}) %all-to-all-start.2) | async-done | bytes 12582944 | tf_op jit(solution)/shard_map/all_to_all | solution.py:52
  419.8 8.1 %convert_reduce_fusion = f32[16,64,2]{2,1,0:T(8,128)S(1)} fusion(bf16[16,64,32,2,96]{4,2,3,1,0:T(8,128)(2,1)} %all-to-all-done.2), kind=kLoop, calls=%fused_computation.2 | loop fusion | flops 12580864 | bytes 12591104 | tf_op jit(solution)/shard_map/reduce_sum | solution.py:12
  427.9 0.2 copy.42
  428.1 13.9 %fusion.10 = f32[2,64,1024]{2,1,0:T(8,128)} fusion(bf16[1024,32,2,96]{3,1,2,0:T(8,128)(2,1)} %bitcast.5, bf16[64,32,2,96]{3,2,0,1:T(2,128)(2,1)S(1)} %reshape.184, f32[2,1024]{1,0:T(2,128)S(1)} %bitcast.26, f32[2,64]{1,0:T(2,128)S(1)} %bitcast.28, f32[2]{0:T(128)S(1)} %convert_reduce_fusion.3), kind=kOutput, calls=%fused_computation.13 | convolution fusion | flops 805699584 | bytes 13902344 | tf_op jit(solution)/shard_map/tsbc,usbc->btu/dot_general | solution.py:11
  (27 shorter events, 1.1 us)
Async XLA Ops:
  0.0 43.1 %copy-start = (bf16[16,8192]{1,0:T(8,128)(2,1)S(1)}, bf16[16,8192]{1,0:T(8,128)(2,1)}, u32[]{:S(2)}) copy-start(bf16[16,8192]{1,0:T(8,128)(2,1)} %param.6) | copy-start | bytes 786436
  8.8 34.4 %copy-start.1 = (bf16[64,8192]{1,0:T(8,128)(2,1)S(1)}, bf16[64,8192]{1,0:T(8,128)(2,1)}, u32[]{:S(2)}) copy-start(bf16[64,8192]{1,0:T(8,128)(2,1)} %param.5) | copy-start | bytes 3145732
  8.8 34.4 %copy-start.2 = (f32[64,16]{0,1:T(8,128)S(1)}, f32[64,16]{0,1:T(8,128)}, u32[]{:S(2)}) copy-start(f32[64,16]{0,1:T(8,128)} %param.7) | copy-start | bytes 12292
  8.8 34.4 %copy-start.3 = (s32[64]{0:T(128)S(1)}, s32[64]{0:T(128)}, u32[]{:S(2)}) copy-start(s32[64]{0:T(128)} %param.8) | copy-start | bytes 772
  70.4 72.5 %all-to-all-start.1 = ((bf16[64,32,192]{2,0,1:T(8,128)(2,1)}), bf16[64,32,192]{2,0,1:T(8,128)(2,1)S(1)}, u32[]{:S(2)}, u32[]{:S(2)}) async-start(bf16[64,32,192]{2,0,1:T(8,128)(2,1)} %broadcast_select_fusion), calls=%async_computation.1 | async-start | bytes 2097152 | tf_op jit(solution)/shard_map/all_to_all | solution.py:41
  142.8 15.8 %all-to-all-start = ((bf16[1,32,2]{2,0,1:T(2,128)(2,1)}), bf16[1,32,2]{2,0,1:T(2,128)(2,1)S(1)}, u32[]{:S(2)}, u32[]{:S(2)}) async-start(bf16[1,32,2]{2,0,1:T(2,128)(2,1)} %convert_element_type.47), calls=%async_computation | async-start | bytes 32768 | tf_op jit(solution)/shard_map/all_to_all | solution.py:42
  164.9 254.9 %all-to-all-start.2 = ((bf16[16,64,32,2,96]{4,2,3,1,0:T(8,128)(2,1)}), bf16[16,64,32,2,96]{4,2,3,1,0:T(8,128)(2,1)}, u32[]{:S(2)}, u32[]{:S(2)}) async-start(bf16[16,64,32,2,96]{4,2,3,1,0:T(8,128)(2,1)} %stack.3), calls=%async_computation.2 | async-start | bytes 33554432 | tf_op jit(solution)/shard_map/all_to_all | solution.py:52
